TPU v7x, 128 devices: a whole 4x4x4 slice. The times are simulated.
128 devices in a mesh: cfg: 2 (over z_lo), seq: 8 (over x, core), blk: 8 (over z_hi, y).
Axes of the slice: x: 4, y: 4, z: 4 (z_hi: 2, z_lo: 2; z = z_hi * 2 + z_lo), core: 2. Of those that a mesh axis runs over, the one named last changes fastest.
Arguments:
- hidden: bfloat16 [2, 3072, 5120], P('cfg', 'seq', 'blk'), may hold values from -2.5 to 2.5
- modulation: float32 [3, 5120], replicated, may hold values from -4 to 4
- in_projection: bfloat16 [5120, 3, 3072], P(('cfg', 'seq'), None, 'blk'), may hold values from -0.078125 to 0.078125
- out_projection: bfloat16 [3072, 5120], P('blk', ('cfg', 'seq')), may hold values from -0.15625 to 0.15625
- lengths: int32 [5], replicated, may hold values from 1 to 1536, 3072 in all
- positions: int32 [3, 3072], P(None, 'seq'), may hold values from 0 to 63
- guidance: float32 [1], replicated, may hold values from 2 to 5
Outputs:
- guided: float32 [8, 2, 192, 5120], P('seq', 'cfg', None, 'blk')
Inputs may be any that keep to these rules, and one draw needn't show every extreme that they name: The clip lengths sum to 3072 and the longest is exactly 1536.
All inputs are finite; a program needn't handle non-finite values.
Results may differ from a plain program's by a relative error of at most 0.012.
The roundings to bfloat16 on the way count: a program that leaves them out, or rounds other values in their place, can miss the bound.
Values may be sent and summed in bfloat16 or wider, within the bound.
A program may use at most 128 MiB of HBM per device.

v0:
```python
import jax
import jax.numpy as jnp
import numpy as np
from jax import lax
from jax.sharding import PartitionSpec as P

HEAD_DIM = 128


def from_partner(array, axis, distance):
    return lax.ppermute(array, axis, [(i, i ^ 1 << distance) for i in range(lax.axis_size(axis))])


def rotary_angles(head_width):
    third = head_width // 6
    first_dim = head_width - 4 * third
    other_dim = 2 * third
    pair_index = np.arange(head_width) // 2
    first_pairs = first_dim // 2
    other_pairs = other_dim // 2
    in_first = pair_index < first_pairs
    in_second = (pair_index >= first_pairs) & (pair_index < first_pairs + other_pairs)
    in_third = pair_index >= first_pairs + other_pairs
    row_first = np.where(in_first, 10000.0 ** (-2.0 * pair_index / first_dim), 0.0)
    row_second = np.where(
        in_second, 10000.0 ** (-2.0 * (pair_index - first_pairs) / other_dim), 0.0
    )
    row_third = np.where(
        in_third, 10000.0 ** (-2.0 * (pair_index - first_pairs - other_pairs) / other_dim), 0.0
    )
    return np.stack([row_first, row_second, row_third]).astype(np.float32)


def turn_matrix(head_width):
    row_index = np.arange(head_width)[:, None]
    col_index = np.arange(head_width)[None, :]
    upper = np.where((col_index == row_index + 1) & (row_index % 2 == 0), 1.0, 0.0)
    lower = np.where((col_index == row_index - 1) & (row_index % 2 == 1), -1.0, 0.0)
    return (upper + lower).astype(np.float32)


def layer_norm(inputs):
    row_mean = jnp.mean(inputs, -1, keepdims=True)
    centered = inputs - row_mean
    variance = jnp.mean(centered * centered, -1, keepdims=True)
    return centered * lax.rsqrt(variance + 1e-06)


def rms_norm(inputs):
    return inputs * lax.rsqrt(jnp.mean(inputs * inputs, -1, keepdims=True) + 1e-06)


def rotate(inputs, cosine, sine, turning):
    turned = jnp.einsum("thd,de->the", inputs, turning, precision=lax.Precision.HIGHEST)
    return inputs * cosine + turned * sine


def clip_index(clip_ends, first_row, count):
    token_index = first_row + jnp.arange(count, dtype=jnp.int32)
    return jnp.sum((token_index[:, None] >= clip_ends[None, :]).astype(jnp.int32), 1)


def local(hidden, modulation, in_projection, out_projection, lengths, positions, guidance):
    states = hidden[0]
    tok_count = states.shape[0]
    feat_width = states.shape[1]
    half_rows = tok_count // 2
    inner_width = in_projection.shape[2]
    head_count = inner_width // HEAD_DIM
    full_states = lax.all_gather(states, "blk", axis=1, tiled=True)
    modulated = (
        layer_norm(full_states.astype(jnp.float32)) * (1.0 + modulation[1]) + modulation[0]
    ).astype(jnp.bfloat16)
    piece = lax.all_gather(in_projection, ("cfg", "seq"), axis=0, tiled=True)
    mixed = jnp.dot(
        modulated,
        piece.reshape(piece.shape[0], 3 * inner_width),
        preferred_element_type=jnp.float32,
    )
    mixed = mixed.reshape(tok_count, 3, head_count, HEAD_DIM)
    angle_table = jnp.asarray(rotary_angles(HEAD_DIM))
    turning = jnp.asarray(turn_matrix(HEAD_DIM))
    angles = jnp.einsum(
        "at,ae->te", positions.astype(jnp.float32), angle_table, precision=lax.Precision.HIGHEST
    )
    cosine = jnp.cos(angles)[:, None, :]
    sine = jnp.sin(angles)[:, None, :]
    queries = rotate(rms_norm(mixed[:, 0]), cosine, sine, turning).astype(jnp.bfloat16)
    key_rows = rotate(rms_norm(mixed[:, 1]), cosine, sine, turning).astype(jnp.bfloat16)
    value_rows = mixed[:, 2].astype(jnp.bfloat16)
    clip_ends = jnp.cumsum(lengths)
    query_clip = clip_index(clip_ends, lax.axis_index("seq") * tok_count, tok_count)
    score_scale = HEAD_DIM ** (-0.5)
    start_state = (
        jnp.zeros((tok_count, head_count, HEAD_DIM), jnp.float32),
        jnp.zeros((head_count, tok_count), jnp.float32),
    )
    first_row = jnp.int32(0)
    key_piece = lax.all_gather(key_rows, "seq", axis=0, tiled=True)
    value_piece = lax.all_gather(value_rows, "seq", axis=0, tiled=True)
    row_count = key_piece.shape[0]
    key_block = 512 if row_count % 512 == 0 else row_count

    def key_step(block_index, running):
        numerator, denominator = running
        key_slab = lax.dynamic_slice_in_dim(key_piece, block_index * key_block, key_block, 0)
        value_slab = lax.dynamic_slice_in_dim(value_piece, block_index * key_block, key_block, 0)
        key_clip = clip_index(clip_ends, first_row + block_index * key_block, key_block)
        scores = (
            jnp.einsum("qhd,khd->hqk", queries, key_slab, preferred_element_type=jnp.float32)
            * score_scale
        )
        same_clip = query_clip[:, None] == key_clip[None, :]
        weights = jnp.where(same_clip[None], jnp.exp(scores), 0.0)
        numerator = numerator + jnp.einsum(
            "hqk,khd->qhd",
            weights.astype(jnp.bfloat16),
            value_slab,
            preferred_element_type=jnp.float32,
        )
        denominator = denominator + jnp.sum(weights, -1)
        return (numerator, denominator)

    numerator, denominator = lax.fori_loop(0, row_count // key_block, key_step, start_state)
    attended = (
        (numerator / jnp.transpose(denominator)[:, :, None])
        .astype(jnp.bfloat16)
        .reshape(tok_count, inner_width)
    )
    col_start = lax.axis_index("blk") * feat_width
    own_inputs = states.astype(jnp.float32)
    cfg_index = lax.axis_index("cfg")
    partial_out = jnp.dot(
        attended,
        lax.all_gather(out_projection, ("cfg", "seq"), axis=1, tiled=True),
        preferred_element_type=jnp.float32,
    )
    projected = lax.psum_scatter(partial_out, "blk", scatter_dimension=1, tiled=True)
    gate_vector = lax.dynamic_slice_in_dim(modulation[2], col_start, feat_width, 0)
    block_out = own_inputs + gate_vector * projected
    other_out = from_partner(block_out, "cfg", 0)
    mine_rows = lax.dynamic_slice_in_dim(block_out, cfg_index * half_rows, half_rows, 0)
    their_rows = lax.dynamic_slice_in_dim(other_out, cfg_index * half_rows, half_rows, 0)
    is_cond = cfg_index == 0
    cond_rows = jnp.where(is_cond, mine_rows, their_rows)
    uncond_rows = jnp.where(is_cond, their_rows, mine_rows)
    guided = uncond_rows + guidance[0] * (cond_rows - uncond_rows)
    return guided.reshape(1, 1, half_rows, feat_width)


def solution(mesh):
    return jax.shard_map(
        local,
        mesh=mesh,
        in_specs=(
            P("cfg", "seq", "blk"),
            P(),
            P(("cfg", "seq"), None, "blk"),
            P("blk", ("cfg", "seq")),
            P(),
            P(None, "seq"),
            P(),
        ),
        out_specs=P("seq", "cfg", None, "blk"),
        check_vma=False,
    )
```

profile of v0, /device:TPU:0, one launch (start us, length us, event | category | flops | bytes accessed | tf_op | source)
XLA Modules:
  0.0 421.1 jit_solution(1140254993012736413)
XLA Ops:
  6.5 0.0 all-gather.14.cloned.1.call-start
  6.5 0.7 all-gather.14.cloned.1.call-update
  7.3 0.0 all-gather.8.cloned.1.call-start
  7.3 0.7 all-gather.8.cloned.1.call-update
  8.0 0.0 all-gather.16.cloned.1.call-start
  8.1 1.1 fusion.38
  9.2 72.2 %all-gather.14.cloned.1.call-done = bf16[1,384,5120]{2,1,0:T(8,128)(2,1)} async-done(((bf16[1,384,640]{2,1,0:T(8,128)(2,1)}), bf16[1,384,5120]{2,1,0:T(8,128)(2,1)}) %all-gather.14.cloned.1.call-update) | async-done | bytes 3932176 | tf_op jit(solution)/shard_map/all_gather | solution.py:70
  81.3 2.9 convert_reduce_fusion.1
  84.2 0.4 copy-done
  84.6 1.2 fusion.17
  85.8 63.0 %all-gather.8.cloned.1.call-done = bf16[5120,3,384]{2,0,1:T(8,128)(2,1)} async-done(((bf16[320,3,384]{2,0,1:T(8,128)(2,1)}), bf16[5120,3,384]{2,0,1:T(8,128)(2,1)}) %all-gather.8.cloned.1.call-update) | async-done | bytes 11796496 | tf_op jit(solution)/shard_map/all_gather | solution.py:74
  148.8 16.2 %copy.34 = bf16[5120,3,384]{0,2,1:T(8,128)(2,1)} copy(bf16[5120,3,384]{2,0,1:T(8,128)(2,1)} %all-gather.8.cloned.1.call-done) | data formatting | bytes 23592960 | tf_op jit(solution)/shard_map/all_gather | solution.py:74
  165.1 10.7 %fusion.22 = f32[384,3,3,128]{0,3,2,1:T(8,128)S(1)} fusion(bf16[3,3,128,5120]{3,2,1,0:T(8,128)(2,1)} %bitcast.94, bf16[1,384,5120]{2,1,0:T(8,128)(2,1)} %all-gather.14.cloned.1.call-done, f32[5120]{0:T(1024)S(1)} %bitcast.98, f32[5120]{0:T(1024)S(1)} %bitcast.99, f32[384]{0:T(512)S(1)} %add_rsqrt_fusion.2, f32[384]{0:T(512)S(1)} %broadcast_multiply_fusion), kind=kOutput, calls=%fused_computation.29 | convolution fusion | flops 4541644800 | bytes 17542144 | tf_op jit(solution)/shard_map/dot_general | solution.py:75
  175.7 0.0 copy-start.5
  175.7 0.7 slice.48
  176.5 0.0 all-gather.16.cloned.1.call-update
  176.5 0.0 all-gather.10.cloned.1.call-start
  176.6 1.1 cosine_bitcast_fusion
  177.7 0.1 multiply_reduce_fusion
  177.8 1.4 fusion.30
  179.2 0.0 all-gather.10.cloned.1.call-update
  179.2 0.0 all-gather.12.cloned.1.call-start
  179.3 0.5 all-gather.12.cloned.1.call-update
  179.8 0.2 reduce-scatter.2.cloned.1.call-start
  180.1 0.2 reduce-window.8
  180.3 0.1 convert_reduce_fusion.2
  180.3 0.7 fusion.31
  181.0 0.2 copy.40
  181.3 22.3 %all-gather.16.cloned.1.call-done = bf16[3072,1,3,128]{0,3,2,1:T(8,128)(2,1)} async-done(((bf16[384,1,3,128]{0,3,2,1:T(8,128)(2,1)}), bf16[3072,1,3,128]{0,3,2,1:T(8,128)(2,1)}) %all-gather.16.cloned.1.call-update) | async-done | bytes 2359312 | tf_op jit(solution)/shard_map/all_gather | solution.py:100
  203.6 27.7 %all-gather.10.cloned.1.call-done = bf16[3072,3,128]{0,2,1:T(8,128)(2,1)} async-done(((bf16[384,3,128]{0,2,1:T(8,128)(2,1)}), bf16[3072,3,128]{0,2,1:T(8,128)(2,1)}) %all-gather.10.cloned.1.call-update) | async-done | bytes 2359312 | tf_op jit(solution)/shard_map/all_gather | solution.py:99
  231.3 22.9 %while.16 = (s32[]{:T(128)}, f32[384,3,128]{0,2,1:T(8,128)S(1)}, f32[3,384]{1,0:T(4,128)S(1)}, bf16[3072,3,128]{0,2,1:T(8,128)(2,1)}, s32[384]{0:T(512)S(1)}, /*...) while((s32[]{:T(128)}, f32[384,3,128]{0,2,1:T(8,128)S(1)}, ...), condition=%wide.region_9.10_spmd.clone, body=%wide.region_6.9_spmd.clone.sunk | while | flops 306029184 | bytes 7597782 | solution.py:124
  231.3 0.1 convert_reduce_fusion.4
  231.4 0.2 broadcast_compare_fusion.2
  231.6 1.8 fusion.57
  233.4 1.7 fusion.58
  235.1 0.1 convert_reduce_fusion.4
  235.2 0.2 broadcast_compare_fusion.2
  235.4 1.8 fusion.57
  237.2 1.7 fusion.58
  238.9 0.1 convert_reduce_fusion.4
  239.0 0.2 broadcast_compare_fusion.2
  239.2 1.8 fusion.57
  241.0 1.7 fusion.58
  242.7 0.1 convert_reduce_fusion.4
  242.8 0.2 broadcast_compare_fusion.2
  243.0 1.8 fusion.57
  244.8 1.7 fusion.58
  246.6 0.1 convert_reduce_fusion.4
  246.6 0.2 broadcast_compare_fusion.2
  246.8 1.9 fusion.57
  248.7 1.7 fusion.58
  250.4 0.1 convert_reduce_fusion.4
  250.5 0.2 broadcast_compare_fusion.2
  250.6 1.9 fusion.57
  252.5 1.7 fusion.58
  254.2 0.1 divide_convert_fusion
  254.3 15.6 %all-gather.12.cloned.1.call-done = bf16[384,5120]{0,1:T(8,128)(2,1)} async-done(((bf16[384,320]{0,1:T(8,128)(2,1)}), bf16[384,5120]{0,1:T(8,128)(2,1)}) %all-gather.12.cloned.1.call-update) | async-done | bytes 3932176 | tf_op jit(solution)/shard_map/all_gather | solution.py:135
  269.9 7.4 %fusion.41 = f32[384,5120]{1,0:T(8,128)} fusion(bf16[384,384]{0,1:T(8,128)(2,1)S(1)} %bitcast.96, bf16[384,5120]{0,1:T(8,128)(2,1)} %all-gather.12.cloned.1.call-done), kind=kOutput, calls=%fused_computation.65 | convolution fusion | flops 1509949440 | bytes 12091392 | tf_op jit(solution)/shard_map/dot_general | solution.py:133
  277.3 0.0 reduce-scatter.2.cloned.1.call-update
  277.4 111.9 %reduce-scatter.2.cloned.1.call-done = f32[384,640]{1,0:T(8,128)} async-done(((f32[384,5120]{1,0:T(8,128)}), f32[384,640]{1,0:T(8,128)}) %reduce-scatter.2.cloned.1.call-update) | async-done | bytes 983056 | tf_op jit(solution)/shard_map/reduce_scatter | solution.py:138
  389.3 1.3 convert_add_fusion
  390.6 0.7 collective-permute-start
  392.0 21.4 %collective-permute-done = f32[384,640]{1,0:T(8,128)S(1)} collective-permute-done((f32[384,640]{1,0:T(8,128)S(1)}, f32[384,640]{1,0:T(8,128)S(1)}, u32[]{:S(2)}, u32[]{:S(2)}) %collective-permute-start) | collective-permute-done | bytes 983072 | tf_op jit(solution)/shard_map/ppermute | solution.py:11
  413.3 0.9 add_bitcast_fusion
  (30 shorter events, 0.2 us)
Async XLA Ops:
  6.5 74.8 %all-gather.14.cloned.1.call-start = ((), (), s32[]{:S(2)}) async-start(), calls=%async_computation.5 | async-start | bytes 4423680 | tf_op jit(solution)/shard_map/all_gather | solution.py:70
  7.3 141.6 %all-gather.8.cloned.1.call-start = ((), (), s32[]{:S(2)}) async-start(), calls=%async_computation.1 | async-start | bytes 12533760 | tf_op jit(solution)/shard_map/all_gather | solution.py:74
  8.0 195.6 %all-gather.16.cloned.1.call-start = ((), (), s32[]{:S(2)}) async-start(), calls=%async_computation.6 | async-start | bytes 2654208 | tf_op jit(solution)/shard_map/all_gather | solution.py:100
  81.3 3.3 copy-start
  165.0 11.5 %copy-start.3 = (s32[3,384]{1,0:T(4,128)S(1)}, s32[3,384]{1,0:T(4,128)}, u32[]{:S(2)}) copy-start(s32[3,384]{1,0:T(4,128)} %param.16) | copy-start | bytes 13828
  165.0 11.5 %copy-start.4 = (f32[3,128]{1,0:T(4,128)S(1)}, f32[3,128]{1,0:T(4,128)}, u32[]{:S(2)}) copy-start(f32[3,128]{1,0:T(4,128)} %constant.88.clone) | copy-start | bytes 4612
  165.1 12.7 %copy-start.2 = (f32[128,128,1]{1,0,2:T(8,128)S(1)}, f32[128,128,1]{1,0,2:T(8,128)}, u32[]{:S(2)}) copy-start(f32[128,128,1]{1,0,2:T(8,128)} %constant.91) | copy-start | bytes 196612
  175.7 4.3 %copy-start.5 = (s32[5]{0:T(128)S(1)}, s32[5]{0:T(128)}, u32[]{:S(2)}) copy-start(s32[5]{0:T(128)} %param.15) | copy-start | bytes 64
  176.5 54.8 %all-gather.10.cloned.1.call-start = ((), (), s32[]{:S(2)}) async-start(), calls=%async_computation.2 | async-start | bytes 2654208 | tf_op jit(solution)/shard_map/all_gather | solution.py:99
  179.2 90.7 %all-gather.12.cloned.1.call-start = ((), (), s32[]{:S(2)}) async-start(), calls=%async_computation.3 | async-start | bytes 4177920 | tf_op jit(solution)/shard_map/all_gather | solution.py:135
  179.8 209.5 %reduce-scatter.2.cloned.1.call-start = ((), (), s32[]{:S(2)}) async-start(), calls=%async_computation.4 | async-start | bytes 8847360 | tf_op jit(solution)/shard_map/reduce_scatter | solution.py:138
  277.3 112.0 %copy-start.1 = (bf16[1,384,640]{2,1,0:T(8,128)(2,1)S(1)}, bf16[1,384,640]{2,1,0:T(8,128)(2,1)}, u32[]{:S(2)}) copy-start(bf16[1,384,640]{2,1,0:T(8,128)(2,1)} %param.11) | copy-start | bytes 1474564
  390.6 22.8 %collective-permute-start = (f32[384,640]{1,0:T(8,128)S(1)}, f32[384,640]{1,0:T(8,128)S(1)}, u32[]{:S(2)}, u32[]{:S(2)}) collective-permute-start(f32[384,640]{1,0:T(8,128)S(1)} %convert_add_fusion), channel_id=1, source_target_pairs={{0,64},{64,0},{1,65},{65,1},{2,66},{66,2},{3,67},{67,3},{4,68},{68... | collective-permute-start | bytes 2949128 | tf_op jit(solution)/shard_map/ppermute | solution.py:11
Sparse Core Ops, SparseCore 0:
  9.7 71.6 all-gather.13
  83.0 65.7 all-gather.7
  176.6 26.8 all-gather.15
  205.1 26.1 all-gather.9
  232.8 36.9 all-gather.11
  277.5 111.7 reduce-scatter.1
where the time goes:
time: 422 us; the launch traced here: 421 us
  waiting for transfers between devices  336 us (80%)
  matrix products  42.3 us (10%)
  local copies, waits for them, and re-layouts  17.6 us (4%)
  between operations  14.2 us (3%)
  other arithmetic  9.41 us (2%)
    reduce_scatter x1, waiting for transfers between devices, local(): lax.psum_scatter(partial_out, 'blk', scatter_dimension=1, tiled=True)  112 us
    all_gather x1, waiting for transfers between devices, local(): full_states = lax.all_gather(states, 'blk', axis=1, tiled=True)  72.2 us
    all_gather x1, waiting for transfers between devices, local(): piece = lax.all_gather(in_projection, ('cfg', 'seq'), axis=0, tiled=True)  63 us
    all_gather x1, waiting for transfers between devices, local(): key_piece = lax.all_gather(key_rows, 'seq', axis=0, tiled=True)  27.7 us
    all_gather x1, waiting for transfers between devices, local(): value_piece = lax.all_gather(value_rows, 'seq', axis=0, tiled=True)  22.3 us
    ppermute x1, waiting for transfers between devices, from_partner(): lax.ppermute(array, axis, [(i, i ^ 1 << distance) for i in range(lax.axis...  21.4 us
    all_gather x1, local copies, waits for them, and re-layouts, local(): piece = lax.all_gather(in_projection, ('cfg', 'seq'), axis=0, tiled=True)  16.2 us
    all_gather x1, waiting for transfers between devices, local(): lax.all_gather(out_projection, ('cfg', 'seq'), axis=1, tiled=True)  15.6 us
  transfers between devices with their start and end apart: 7, of which 7 were waited for; matrix products, arithmetic and copies ran while one was open for 8% of the time, Pallas kernels for 0%

commit v1 on v0

--- a/solution.py
+++ b/solution.py
@@ -3,6 +3,7 @@
 import numpy as np
 from jax import lax
 from jax.sharding import PartitionSpec as P
+from jax.lax import all_to_all, psum
 
 HEAD_DIM = 128
 
@@ -71,7 +72,13 @@
     modulated = (
         layer_norm(full_states.astype(jnp.float32)) * (1.0 + modulation[1]) + modulation[0]
     ).astype(jnp.bfloat16)
-    piece = lax.all_gather(in_projection, ("cfg", "seq"), axis=0, tiled=True)
+
+    def lay_signs(target):
+        main = jnp.stack([target for _ in range(psum(1, ("cfg", "seq")))], 0)
+        carry_out = all_to_all(main, ("cfg", "seq"), 0, 0)
+        return jnp.concatenate(carry_out, 0)
+
+    piece = lay_signs(in_projection)
     mixed = jnp.dot(
         modulated,
         piece.reshape(piece.shape[0], 3 * inner_width),

time: 422 us -> 491 us (1.16)
  local copies, waits for them, and re-layouts: 17.6 us -> 49.8 us
  waiting for transfers between devices: 336 us -> 367 us
  starting transfers between devices: 1.11 us -> 7.19 us
    all_gather x1, waiting for transfers between devices: 72.2 us -> 168 us  [local(): full_states = lax.all_gather(states, 'blk', axis=1, tiled=True)]
    all_gather x1 -> x0, waiting for transfers between devices: 63 us -> none  [local(): piece = lax.all_gather(in_projection, ('cfg', 'seq'), axis=0, tiled=True)]
    another operation x0 -> x2, local copies, waits for them, and re-layouts: none -> 30.3 us  [the longest x1 22.9 us: local(): piece.reshape(piece.shape[0], 3 * inner_width)]
    all_to_all x0 -> x1, local copies, waits for them, and re-layouts: none -> 18.1 us  [lay_signs(): carry_out = all_to_all(main, ('cfg', 'seq'), 0, 0)]
    all_gather x1 -> x0, local copies, waits for them, and re-layouts: 16.2 us -> none  [local(): piece = lax.all_gather(in_projection, ('cfg', 'seq'), axis=0, tiled=True)]
    all_to_all x0 -> x1, starting transfers between devices: none -> 6.05 us  [lay_signs(): carry_out = all_to_all(main, ('cfg', 'seq'), 0, 0)]
  transfers between devices with their start and end apart: 7 -> 7, of which waited for: 7 -> 6; matrix products, arithmetic and copies ran while one was open for 8% -> 6% of each run, Pallas kernels for 0% -> 0%
where the time goes in v1:
time: 491 us; the launch traced here: 489 us
  waiting for transfers between devices  367 us (75%)
  local copies, waits for them, and re-layouts  49.8 us (10%)
  matrix products  42 us (9%)
  between operations  14 us (3%)
  other arithmetic  8.35 us (2%)
  starting transfers between devices  7.19 us (1%)
    all_gather x1, waiting for transfers between devices, local(): full_states = lax.all_gather(states, 'blk', axis=1, tiled=True)  168 us
    reduce_scatter x1, waiting for transfers between devices, local(): lax.psum_scatter(partial_out, 'blk', scatter_dimension=1, tiled=True)  112 us
    all_gather x1, waiting for transfers between devices, local(): key_piece = lax.all_gather(key_rows, 'seq', axis=0, tiled=True)  27.9 us
    another operation x1, local copies, waits for them, and re-layouts, local(): piece.reshape(piece.shape[0], 3 * inner_width)  22.9 us
    ppermute x1, waiting for transfers between devices, from_partner(): lax.ppermute(array, axis, [(i, i ^ 1 << distance) for i in range(lax.axis...  21.4 us
    all_gather x1, waiting for transfers between devices, local(): value_piece = lax.all_gather(value_rows, 'seq', axis=0, tiled=True)  21.3 us
    all_to_all x1, local copies, waits for them, and re-layouts, lay_signs(): carry_out = all_to_all(main, ('cfg', 'seq'), 0, 0)  18.1 us
    all_gather x1, waiting for transfers between devices, local(): lax.all_gather(out_projection, ('cfg', 'seq'), axis=1, tiled=True)  15.6 us
  transfers between devices with their start and end apart: 7, of which 6 were waited for; matrix products, arithmetic and copies ran while one was open for 6% of the time, Pallas kernels for 0%

profile of v1, /device:TPU:0, one launch (start us, length us, event | category | flops | bytes accessed | tf_op | source)
XLA Modules:
  0.0 488.8 jit_solution(8324132556686049197)
XLA Ops:
  6.5 7.4 %stack.2 = bf16[16,320,3,384]{3,1,2,0:T(8,128)(2,1)} broadcast(bf16[320,3,384]{2,0,1:T(8,128)(2,1)} %param.13), dimensions={1,2,3} | broadcast | bytes 12533760 | tf_op jit(solution)/shard_map/stack | solution.py:77
  13.9 6.0 %all-to-all-start = ((bf16[16,320,3,384]{3,1,2,0:T(8,128)(2,1)}), bf16[16,320,3,384]{3,1,2,0:T(8,128)(2,1)}, u32[]{:S(2)}, u32[]{:S(2)}) async-start(bf16[16,320,3,384]{3,1,2,0:T(8,128)(2,1)} %stack.2), calls=%async_computation | async-start | bytes 23592960 | tf_op jit(solution)/shard_map/all_to_all | solution.py:78
  20.0 0.0 all-gather.11.cloned.1.call-start
  20.0 0.7 all-gather.11.cloned.1.call-update
  20.7 0.0 all-gather.13.cloned.1.call-start
  20.8 168.0 %all-gather.11.cloned.1.call-done = bf16[1,384,5120]{2,1,0:T(8,128)(2,1)} async-done(((bf16[1,384,640]{2,1,0:T(8,128)(2,1)}), bf16[1,384,5120]{2,1,0:T(8,128)(2,1)}) %all-gather.11.cloned.1.call-update) | async-done | bytes 3932176 | tf_op jit(solution)/shard_map/all_gather | solution.py:71
  188.8 2.9 convert_reduce_fusion.1
  191.7 0.4 copy-done
  192.1 1.2 fusion.17
  193.3 0.0 all-to-all-done
  193.3 18.1 %copy.35 = bf16[16,320,3,384]{1,0,3,2:T(8,128)(2,1)} copy(bf16[16,320,3,384]{3,1,2,0:T(8,128)(2,1)} %all-to-all-done) | data formatting | bytes 23592960 | tf_op jit(solution)/shard_map/all_to_all | solution.py:78
  211.4 22.9 %reshape_reshape.3 = bf16[5120,1152]{0,1:T(8,128)(2,1)} reshape(bf16[16,320,3,384]{1,0,3,2:T(8,128)(2,1)} %copy.35) | data formatting | bytes 23592960 | tf_op jit(solution)/shard_map/reshape;reshape | solution.py:84
  234.3 10.7 %fusion.22 = f32[384,3,3,128]{0,3,2,1:T(8,128)S(1)} fusion(bf16[3,3,128,5120]{3,2,1,0:T(8,128)(2,1)} %bitcast.96, bf16[1,384,5120]{2,1,0:T(8,128)(2,1)} %all-gather.11.cloned.1.call-done, f32[5120]{0:T(1024)S(1)} %bitcast.100, f32[5120]{0:T(1024)S(1)} %bitcast.101, f32[384]{0:T(512)S(1)} %add_rsqrt_fusion.2, f32[384]{0:T(512)S(1)} %broadcast_multiply_fusion), kind=kOutput, calls=%fused_computation.29 | convolution fusion | flops 4541644800 | bytes 17542144 | tf_op jit(solution)/shard_map/dot_general | solution.py:82
  244.9 0.0 copy-start.6
  244.9 0.7 slice.48
  245.7 0.0 all-gather.13.cloned.1.call-update
  245.7 0.0 all-gather.7.cloned.1.call-start
  245.8 1.1 cosine_bitcast_fusion
  246.9 0.1 multiply_reduce_fusion
  247.0 1.4 fusion.30
  248.4 0.0 all-gather.7.cloned.1.call-update
  248.4 0.0 all-gather.9.cloned.1.call-start
  248.5 0.5 all-gather.9.cloned.1.call-update
  249.0 0.2 reduce-scatter.2.cloned.1.call-start
  249.3 0.2 reduce-window.8
  249.5 0.1 convert_reduce_fusion.2
  249.5 0.7 fusion.31
  250.2 0.2 copy.41
  250.5 21.3 %all-gather.13.cloned.1.call-done = bf16[3072,1,3,128]{0,3,2,1:T(8,128)(2,1)} async-done(((bf16[384,1,3,128]{0,3,2,1:T(8,128)(2,1)}), bf16[3072,1,3,128]{0,3,2,1:T(8,128)(2,1)}) %all-gather.13.cloned.1.call-update) | async-done | bytes 2359312 | tf_op jit(solution)/shard_map/all_gather | solution.py:107
  271.8 27.9 %all-gather.7.cloned.1.call-done = bf16[3072,3,128]{0,2,1:T(8,128)(2,1)} async-done(((bf16[384,3,128]{0,2,1:T(8,128)(2,1)}), bf16[3072,3,128]{0,2,1:T(8,128)(2,1)}) %all-gather.7.cloned.1.call-update) | async-done | bytes 2359312 | tf_op jit(solution)/shard_map/all_gather | solution.py:106
  299.7 22.7 %while.16 = (s32[]{:T(128)}, f32[384,3,128]{0,2,1:T(8,128)S(1)}, f32[3,384]{1,0:T(4,128)S(1)}, bf16[3072,3,128]{0,2,1:T(8,128)(2,1)}, s32[384]{0:T(512)S(1)}, /*...) while((s32[]{:T(128)}, f32[384,3,128]{0,2,1:T(8,128)S(1)}, ...), condition=%wide.region_9.10_spmd.clone, body=%wide.region_6.9_spmd.clone.sunk | while | flops 306029184 | bytes 7597782 | solution.py:131
  299.7 0.1 convert_reduce_fusion.4
  299.8 0.2 broadcast_compare_fusion.2
  300.0 1.8 fusion.57
  301.8 1.6 fusion.58
  303.5 0.1 convert_reduce_fusion.4
  303.5 0.2 broadcast_compare_fusion.2
  303.7 1.8 fusion.57
  305.6 1.6 fusion.58
  307.2 0.1 convert_reduce_fusion.4
  307.3 0.2 broadcast_compare_fusion.2
  307.5 1.8 fusion.57
  309.3 1.6 fusion.58
  311.0 0.1 convert_reduce_fusion.4
  311.1 0.2 broadcast_compare_fusion.2
  311.3 1.8 fusion.57
  313.1 1.6 fusion.58
  314.8 0.1 convert_reduce_fusion.4
  314.9 0.2 broadcast_compare_fusion.2
  315.1 1.8 fusion.57
  316.9 1.6 fusion.58
  318.6 0.1 convert_reduce_fusion.4
  318.7 0.2 broadcast_compare_fusion.2
  318.9 1.8 fusion.57
  320.7 1.6 fusion.58
  322.4 0.1 divide_convert_fusion
  322.4 15.6 %all-gather.9.cloned.1.call-done = bf16[384,5120]{0,1:T(8,128)(2,1)} async-done(((bf16[384,320]{0,1:T(8,128)(2,1)}), bf16[384,5120]{0,1:T(8,128)(2,1)}) %all-gather.9.cloned.1.call-update) | async-done | bytes 3932176 | tf_op jit(solution)/shard_map/all_gather | solution.py:142
  338.1 7.4 %fusion.41 = f32[384,5120]{1,0:T(8,128)} fusion(bf16[384,384]{0,1:T(8,128)(2,1)S(1)} %bitcast.98, bf16[384,5120]{0,1:T(8,128)(2,1)} %all-gather.9.cloned.1.call-done), kind=kOutput, calls=%fused_computation.65 | convolution fusion | flops 1509949440 | bytes 12091392 | tf_op jit(solution)/shard_map/dot_general | solution.py:140
  345.5 0.0 reduce-scatter.2.cloned.1.call-update
  345.6 111.7 %reduce-scatter.2.cloned.1.call-done = f32[384,640]{1,0:T(8,128)} async-done(((f32[384,5120]{1,0:T(8,128)}), f32[384,640]{1,0:T(8,128)}) %reduce-scatter.2.cloned.1.call-update) | async-done | bytes 983056 | tf_op jit(solution)/shard_map/reduce_scatter | solution.py:145
  457.3 1.3 convert_add_fusion
  458.6 0.8 collective-permute-start
  460.0 21.4 %collective-permute-done = f32[384,640]{1,0:T(8,128)S(1)} collective-permute-done((f32[384,640]{1,0:T(8,128)S(1)}, f32[384,640]{1,0:T(8,128)S(1)}, u32[]{:S(2)}, u32[]{:S(2)}) %collective-permute-start) | collective-permute-done | bytes 983072 | tf_op jit(solution)/shard_map/ppermute | solution.py:12
  481.4 0.9 add_bitcast_fusion
  (33 shorter events, 0.2 us)
Async XLA Ops:
  13.9 6.8 %copy-start.3 = (f32[3,5120]{1,0:T(4,128)S(1)}, f32[3,5120]{1,0:T(4,128)}, u32[]{:S(2)}) copy-start(f32[3,5120]{1,0:T(4,128)} %param.12) | copy-start | bytes 184324
  13.9 179.3 %all-to-all-start = ((bf16[16,320,3,384]{3,1,2,0:T(8,128)(2,1)}), bf16[16,320,3,384]{3,1,2,0:T(8,128)(2,1)}, u32[]{:S(2)}, u32[]{:S(2)}) async-start(bf16[16,320,3,384]{3,1,2,0:T(8,128)(2,1)} %stack.2), calls=%async_computation | async-start | bytes 23592960 | tf_op jit(solution)/shard_map/all_to_all | solution.py:78
  20.0 168.8 %all-gather.11.cloned.1.call-start = ((), (), s32[]{:S(2)}) async-start(), calls=%async_computation.5 | async-start | bytes 4423680 | tf_op jit(solution)/shard_map/all_gather | solution.py:71
  20.7 251.1 %all-gather.13.cloned.1.call-start = ((), (), s32[]{:S(2)}) async-start(), calls=%async_computation.6 | async-start | bytes 2654208 | tf_op jit(solution)/shard_map/all_gather | solution.py:107
  188.8 3.3 copy-start
  234.2 11.5 %copy-start.4 = (s32[3,384]{1,0:T(4,128)S(1)}, s32[3,384]{1,0:T(4,128)}, u32[]{:S(2)}) copy-start(s32[3,384]{1,0:T(4,128)} %param.16) | copy-start | bytes 13828
  234.3 11.5 %copy-start.5 = (f32[3,128]{1,0:T(4,128)S(1)}, f32[3,128]{1,0:T(4,128)}, u32[]{:S(2)}) copy-start(f32[3,128]{1,0:T(4,128)} %constant.88.clone) | copy-start | bytes 4612
  234.3 12.7 %copy-start.2 = (f32[128,128,1]{1,0,2:T(8,128)S(1)}, f32[128,128,1]{1,0,2:T(8,128)}, u32[]{:S(2)}) copy-start(f32[128,128,1]{1,0,2:T(8,128)} %constant.91) | copy-start | bytes 196612
  244.9 4.3 copy-start.6
  245.7 54.0 %all-gather.7.cloned.1.call-start = ((), (), s32[]{:S(2)}) async-start(), calls=%async_computation.2 | async-start | bytes 2654208 | tf_op jit(solution)/shard_map/all_gather | solution.py:106
  248.4 89.7 %all-gather.9.cloned.1.call-start = ((), (), s32[]{:S(2)}) async-start(), calls=%async_computation.3 | async-start | bytes 4177920 | tf_op jit(solution)/shard_map/all_gather | solution.py:142
  249.0 208.3 %reduce-scatter.2.cloned.1.call-start = ((), (), s32[]{:S(2)}) async-start(), calls=%async_computation.4 | async-start | bytes 8847360 | tf_op jit(solution)/shard_map/reduce_scatter | solution.py:145
  345.5 111.8 %copy-start.1 = (bf16[1,384,640]{2,1,0:T(8,128)(2,1)S(1)}, bf16[1,384,640]{2,1,0:T(8,128)(2,1)}, u32[]{:S(2)}) copy-start(bf16[1,384,640]{2,1,0:T(8,128)(2,1)} %param.11) | copy-start | bytes 1474564
  458.6 22.8 %collective-permute-start = (f32[384,640]{1,0:T(8,128)S(1)}, f32[384,640]{1,0:T(8,128)S(1)}, u32[]{:S(2)}, u32[]{:S(2)}) collective-permute-start(f32[384,640]{1,0:T(8,128)S(1)} %convert_add_fusion), channel_id=1, source_target_pairs={{0,64},{64,0},{1,65},{65,1},{2,66},{66,2},{3,67},{67,3},{4,68},{68... | collective-permute-start | bytes 2949128 | tf_op jit(solution)/shard_map/ppermute | solution.py:12
Sparse Core Ops, SparseCore 0:
  23.1 165.6 all-gather.10
  245.8 25.9 all-gather.12
  273.5 26.1 all-gather.6
  301.2 36.7 all-gather.8
  345.7 111.5 reduce-scatter.1
